TPU v7x, 32 devices: a whole 2x2x4 slice. The times are simulated.
32 devices in a mesh: groups: 2 (over y), res: 4 (over z), col: 2 (over x), seq: 2 (over core).
Axes of the slice: x: 2, y: 2, z: 4, core: 2. Of those that a mesh axis runs over, the one named last changes fastest.
Arguments:
- alignment_states: bfloat16 [128, 128, 256], P(('groups', 'res', 'seq'), 'col'), parts along dimension 0, may hold values from -6 to 6
- standardize_scale: float32 [256], replicated, may hold values from 0.5 to 1.5
- standardize_shift: float32 [256], replicated, may hold values from -3 to 3
- first_factor_coeffs: bfloat16 [256, 32], replicated, may hold values from -0.375 to 0.375
- first_factor_offset: float32 [32], replicated, may hold values from -3 to 3
- second_factor_coeffs: bfloat16 [256, 32], replicated, may hold values from -0.375 to 0.375
- second_factor_offset: float32 [32], replicated, may hold values from -3 to 3
- final_coeffs: bfloat16 [1024, 128], replicated, may hold values from -0.1875 to 0.1875
- final_offset: float32 [128], replicated, may hold values from -3 to 3
Outputs:
- pair: bfloat16 [4, 64, 128, 128], P('groups', ('res', 'seq'), 'col'), parts along dimension 0
There are 2 independent parts, one for each index of `groups`. A program takes and returns all parts, laid end to end along the dimension named above; an argument that names none is the same for every part. Nothing has to cross between parts.
All inputs are finite; a program needn't handle non-finite values.
Results may differ from a plain program's by a relative error of at most 0.0037.
Values may be sent and summed in bfloat16 or wider, within the bound.
A program may use at most 64 MiB of HBM per device.

v0:
```python
import jax
import jax.numpy as jnp
from jax import lax
from jax.sharding import PartitionSpec as P


def project_both(rows, standardize_scale, standardize_shift, w_both, bias_both):
    input_tensor = rows.astype(jnp.float32)
    mean = jnp.mean(input_tensor, axis=-1, keepdims=True)
    centred = input_tensor - mean
    variance = jnp.mean(centred * centred, axis=-1, keepdims=True)
    normed = (centred * lax.rsqrt(variance + 1e-05) * standardize_scale + standardize_shift).astype(
        jnp.bfloat16
    )
    return (jnp.dot(normed, w_both, preferred_element_type=jnp.float32) + bias_both).astype(
        jnp.bfloat16
    )


def per_device(
    alignment_states,
    standardize_scale,
    standardize_shift,
    first_factor_coeffs,
    first_factor_offset,
    second_factor_coeffs,
    second_factor_offset,
    final_coeffs,
    final_offset,
):
    aligned_rows_each_shard, position_span, hidden_dimension = alignment_states.shape
    position_number = lax.axis_size("res")
    n_seq = lax.axis_size("seq")
    n_col = lax.axis_size("col")
    positions_each_shard = position_span // position_number
    chans = first_factor_coeffs.shape[1]
    seq_loc = aligned_rows_each_shard * position_number
    w_both = jnp.concatenate([first_factor_coeffs, second_factor_coeffs], axis=1)
    bias_both = jnp.concatenate([first_factor_offset, second_factor_offset])
    raw = lax.all_to_all(
        alignment_states.reshape(
            aligned_rows_each_shard, position_number, positions_each_shard * hidden_dimension
        ),
        "res",
        split_axis=1,
        concat_axis=0,
        tiled=True,
    )
    both = project_both(
        raw.reshape(seq_loc * positions_each_shard, hidden_dimension),
        standardize_scale,
        standardize_shift,
        w_both,
        bias_both,
    )
    both = both.reshape(seq_loc, positions_each_shard, 2 * chans)
    left_loc = both[:, :, :chans].reshape(seq_loc, positions_each_shard * chans)
    right_three = both[:, :, chans:]
    right_loc = right_three.transpose(1, 0, 2).reshape(positions_each_shard, seq_loc * chans)
    left_use = lax.all_to_all(left_loc, "seq", split_axis=1, concat_axis=0, tiled=True)
    right_use = lax.all_gather(right_loc, "seq", axis=1, tiled=True)
    rows_all = lax.all_gather(left_use, "col", axis=1, tiled=True)
    seqs = rows_all.shape[0]
    per_group = seqs // n_seq
    n_rows = rows_all.shape[1] // chans
    left_four = rows_all.reshape(n_seq, per_group, n_rows, chans)
    pair_width = final_coeffs.shape[1]
    w_deep = jnp.concatenate([final_coeffs] * n_seq, axis=0)

    def one_block(block):
        sub = block.shape[0]
        block = block.reshape(sub, n_seq, per_group, chans)
        outer = jnp.einsum("gsic,jgse->ijgce", left_four, block, preferred_element_type=jnp.float32)
        outer = outer.astype(jnp.bfloat16).reshape(n_rows * sub, n_seq * chans * chans)
        summed = jnp.dot(outer, w_deep, preferred_element_type=jnp.float32)
        return summed.reshape(n_rows, sub, pair_width)

    piece = lax.all_gather(right_use, "res", axis=0, tiled=True)
    count = piece.shape[0]
    sub = 1
    for option in range(1, 17):
        if count % option == 0:
            sub = option
    blocks = piece.reshape(count // sub, sub, piece.shape[1])
    results = lax.map(one_block, blocks)
    summed = results.transpose(1, 0, 2, 3).reshape(n_rows, count, pair_width)
    summed = summed.reshape(n_col, n_rows // n_col, summed.shape[1], pair_width)
    total = float(aligned_rows_each_shard * position_number * n_seq)
    return (summed / total + final_offset).astype(jnp.bfloat16)


def solution(mesh):
    return jax.shard_map(
        per_device,
        mesh=mesh,
        in_specs=(P(("groups", "res", "seq"), "col", None), P(), P(), P(), P(), P(), P(), P(), P()),
        out_specs=P("groups", ("res", "seq"), "col", None),
        check_vma=False,
    )
```

profile of v0, /device:TPU:0, one launch (start us, length us, event | category | flops | bytes accessed | tf_op | source)
XLA Modules:
  0.0 109.3 jit_solution(5657845986276746612)
XLA Ops:
  0.0 1.2 %reshape.58 = bf16[8,4,4096]{2,1,0:T(4,128)(2,1)S(1)} reshape(bf16[8,64,256]{2,1,0:T(8,128)(2,1)} %param.11) | data formatting | bytes 524288 | tf_op jit(solution)/shard_map/reshape | solution.py:41
  1.2 0.9 copy.21
  2.0 6.4 %all-to-all-start = ((bf16[8,4,4096]{2,0,1:T(8,128)(2,1)}), bf16[8,4,4096]{2,0,1:T(8,128)(2,1)S(1)}, u32[]{:S(2)}, u32[]{:S(2)}) async-start(bf16[8,4,4096]{2,0,1:T(8,128)(2,1)} %copy.21), calls=%async_computation | async-start | bytes 524288 | tf_op jit(solution)/shard_map/all_to_all | solution.py:40
  8.4 0.7 pad_maximum_fusion.1
  9.2 1.1 pad_maximum_fusion
  10.2 7.1 %all-to-all-done = bf16[8,4,4096]{2,0,1:T(8,128)(2,1)S(1)} async-done(((bf16[8,4,4096]{2,0,1:T(8,128)(2,1)}), bf16[8,4,4096]{2,0,1:T(8,128)(2,1)S(1)}, u32[]{:S(2)}, u32[]{:S(2)}) %all-to-all-start) | async-done | bytes 262176 | tf_op jit(solution)/shard_map/all_to_all | solution.py:40
  17.6 0.2 multiply_reduce_fusion
  17.9 0.3 fusion.4
  18.6 3.7 %all_to_all.28 = bf16[32,2,256]{2,0,1:T(8,128)(2,1)S(1)} all-to-all(bf16[32,2,256]{2,0,1:T(8,128)(2,1)S(1)} %copy.24), channel_id=1, replica_groups=mesh['groups'=2,'res'=4,'col'=2,'seq'=2] {'seq'}, dimensions={1} | all-to-all | bytes 65536 | tf_op jit(solution)/shard_map/all_to_all | solution.py:60
  22.4 4.6 %all_gather.11 = bf16[64,512]{1,0:T(8,128)(2,1)S(1)} all-gather(bf16[64,256]{1,0:T(8,128)(2,1)S(1)} %bitcast.55), channel_id=1, replica_groups=mesh['groups'=2,'res'=4,'col'=2,'seq'=2] {'col'}, dimensions={1}, use_global_device_ids=true | all-gather | bytes 98304 | tf_op jit(solution)/shard_map/all_gather | solution.py:62
  27.4 1.9 %all_gather.9 = bf16[16,2048]{1,0:T(8,128)(2,1)S(1)} all-gather(bf16[16,1024]{1,0:T(8,128)(2,1)S(1)} %reshape.60), channel_id=1, replica_groups=mesh['groups'=2,'res'=4,'col'=2,'seq'=2] {'seq'}, dimensions={1}, use_global_device_ids=true | all-gather | bytes 98304 | tf_op jit(solution)/shard_map/all_gather | solution.py:61
  29.3 13.8 %all_gather.10 = bf16[64,2048]{1,0:T(8,128)(2,1)S(1)} all-gather(bf16[16,2048]{1,0:T(8,128)(2,1)S(1)} %all_gather.9), channel_id=1, replica_groups=mesh['groups'=2,'res'=4,'col'=2,'seq'=2] {'res'}, dimensions={0}, use_global_device_ids=true | all-gather | bytes 327680 | tf_op jit(solution)/shard_map/all_gather | solution.py:78
  43.1 65.3 %while.10 = (s32[]{:T(128)}, f32[4,16,16,128]{3,2,1,0:T(8,128)S(1)}, bf16[4,16,2048]{2,1,0:T(8,128)(2,1)S(1)}, bf16[2,32,16,32]{3,1,2,0:T(8,128)(2,1)S(1)}, bf16[2048,128]{1,0:T(8,128)(2,1)S(1)}, /*index=5*/s32[]{:T(128)}) while((s32[]{:T(128)}, f32[4,16,16,128]{3,2,1,0:T(8,128)S(1)}, bf16[4,16,2048]{2,1,0:T(8,128)(2,1)S(1)}, ...), condition=%wide.region_3.4_spmd, body=%wide.region_2.3_spmd.sunk | while | flops 168296448 | bytes 7340109 | solution.py:85
  43.1 0.2 reshape.70
  43.3 3.2 %convert_bitcast_fusion.3 = bf16[16,16,2,32,32]{3,4,0,1,2:T(8,128)(2,1)} fusion(bf16[2,32,16,32]{3,1,2,0:T(8,128)(2,1)S(1)} %get-tuple-element.101, bf16[16,2,32,32]{3,2,1,0:T(8,128)(2,1)S(1)} %reshape.70), kind=kOutput, calls=%fused_computation.clone.1 | convolution fusion | flops 34078720 | bytes 1179648 | tf_op jit(solution)/shard_map/while/body/eval_jaxpr/gsic,jgse->ijgce/dot_general | solution.py:73
  46.5 6.4 %copy.36 = bf16[16,16,2,32,32]{4,3,2,1,0:T(8,128)(2,1)} copy(bf16[16,16,2,32,32]{3,4,0,1,2:T(8,128)(2,1)} %convert_bitcast_fusion.3) | data formatting | bytes 2097152 | tf_op jit(solution)/shard_map/while/body/eval_jaxpr/convert_element_type | solution.py:74
  53.0 6.0 %reshape.71 = bf16[16,16,2048]{2,1,0:T(8,128)(2,1)S(1)} reshape(bf16[16,16,2,32,32]{4,3,2,1,0:T(8,128)(2,1)} %copy.36) | data formatting | bytes 2097152 | tf_op jit(solution)/shard_map/reshape.23
  59.0 0.4 fusion.27
  59.4 0.2 reshape.70
  59.6 3.2 %convert_bitcast_fusion.3 = bf16[16,16,2,32,32]{3,4,0,1,2:T(8,128)(2,1)} fusion(bf16[2,32,16,32]{3,1,2,0:T(8,128)(2,1)S(1)} %get-tuple-element.101, bf16[16,2,32,32]{3,2,1,0:T(8,128)(2,1)S(1)} %reshape.70), kind=kOutput, calls=%fused_computation.clone.1 | convolution fusion | flops 34078720 | bytes 1179648 | tf_op jit(solution)/shard_map/while/body/eval_jaxpr/gsic,jgse->ijgce/dot_general | solution.py:73
  62.9 6.4 %copy.36 = bf16[16,16,2,32,32]{4,3,2,1,0:T(8,128)(2,1)} copy(bf16[16,16,2,32,32]{3,4,0,1,2:T(8,128)(2,1)} %convert_bitcast_fusion.3) | data formatting | bytes 2097152 | tf_op jit(solution)/shard_map/while/body/eval_jaxpr/convert_element_type | solution.py:74
  69.3 6.0 %reshape.71 = bf16[16,16,2048]{2,1,0:T(8,128)(2,1)S(1)} reshape(bf16[16,16,2,32,32]{4,3,2,1,0:T(8,128)(2,1)} %copy.36) | data formatting | bytes 2097152 | tf_op jit(solution)/shard_map/reshape.23
  75.3 0.4 fusion.27
  76.0 3.2 %convert_bitcast_fusion.3 = bf16[16,16,2,32,32]{3,4,0,1,2:T(8,128)(2,1)} fusion(bf16[2,32,16,32]{3,1,2,0:T(8,128)(2,1)S(1)} %get-tuple-element.101, bf16[16,2,32,32]{3,2,1,0:T(8,128)(2,1)S(1)} %reshape.70), kind=kOutput, calls=%fused_computation.clone.1 | convolution fusion | flops 34078720 | bytes 1179648 | tf_op jit(solution)/shard_map/while/body/eval_jaxpr/gsic,jgse->ijgce/dot_general | solution.py:73
  79.2 6.4 %copy.36 = bf16[16,16,2,32,32]{4,3,2,1,0:T(8,128)(2,1)} copy(bf16[16,16,2,32,32]{3,4,0,1,2:T(8,128)(2,1)} %convert_bitcast_fusion.3) | data formatting | bytes 2097152 | tf_op jit(solution)/shard_map/while/body/eval_jaxpr/convert_element_type | solution.py:74
  85.6 6.0 %reshape.71 = bf16[16,16,2048]{2,1,0:T(8,128)(2,1)S(1)} reshape(bf16[16,16,2,32,32]{4,3,2,1,0:T(8,128)(2,1)} %copy.36) | data formatting | bytes 2097152 | tf_op jit(solution)/shard_map/reshape.23
  91.6 0.4 fusion.27
  92.3 3.2 %convert_bitcast_fusion.3 = bf16[16,16,2,32,32]{3,4,0,1,2:T(8,128)(2,1)} fusion(bf16[2,32,16,32]{3,1,2,0:T(8,128)(2,1)S(1)} %get-tuple-element.101, bf16[16,2,32,32]{3,2,1,0:T(8,128)(2,1)S(1)} %reshape.70), kind=kOutput, calls=%fused_computation.clone.1 | convolution fusion | flops 34078720 | bytes 1179648 | tf_op jit(solution)/shard_map/while/body/eval_jaxpr/gsic,jgse->ijgce/dot_general | solution.py:73
  95.5 6.4 %copy.36 = bf16[16,16,2,32,32]{4,3,2,1,0:T(8,128)(2,1)} copy(bf16[16,16,2,32,32]{3,4,0,1,2:T(8,128)(2,1)} %convert_bitcast_fusion.3) | data formatting | bytes 2097152 | tf_op jit(solution)/shard_map/while/body/eval_jaxpr/convert_element_type | solution.py:74
  102.0 6.0 %reshape.71 = bf16[16,16,2048]{2,1,0:T(8,128)(2,1)S(1)} reshape(bf16[16,16,2,32,32]{4,3,2,1,0:T(8,128)(2,1)} %copy.36) | data formatting | bytes 2097152 | tf_op jit(solution)/shard_map/reshape.23
  108.0 0.4 fusion.27
  108.5 0.8 add_convert_fusion
  (32 shorter events, 1.6 us)
Async XLA Ops:
  0.0 17.9 %copy-start.4 = (f32[256]{0:T(256)S(1)}, f32[256]{0:T(256)}, u32[]{:S(2)}) copy-start(f32[256]{0:T(256)} %param.12) | copy-start | bytes 3076
  0.0 17.9 %copy-start.3 = (f32[256]{0:T(256)S(1)}, f32[256]{0:T(256)}, u32[]{:S(2)}) copy-start(f32[256]{0:T(256)} %param.13) | copy-start | bytes 3076
  0.0 17.9 %copy-start.2 = (bf16[256,32]{0,1:T(8,128)(2,1)S(1)}, bf16[256,32]{0,1:T(8,128)(2,1)}, u32[]{:S(2)}) copy-start(bf16[256,32]{0,1:T(8,128)(2,1)} %param.14) | copy-start | bytes 49156
  0.0 17.9 %copy-start.1 = (bf16[256,32]{0,1:T(8,128)(2,1)S(1)}, bf16[256,32]{0,1:T(8,128)(2,1)}, u32[]{:S(2)}) copy-start(bf16[256,32]{0,1:T(8,128)(2,1)} %param.16) | copy-start | bytes 49156
  2.0 15.3 %all-to-all-start = ((bf16[8,4,4096]{2,0,1:T(8,128)(2,1)}), bf16[8,4,4096]{2,0,1:T(8,128)(2,1)S(1)}, u32[]{:S(2)}, u32[]{:S(2)}) async-start(bf16[8,4,4096]{2,0,1:T(8,128)(2,1)} %copy.21), calls=%async_computation | async-start | bytes 524288 | tf_op jit(solution)/shard_map/all_to_all | solution.py:40
  43.1 65.4 %copy-start = (f32[128]{0:T(128)S(1)}, f32[128]{0:T(128)}, u32[]{:S(2)}) copy-start(f32[128]{0:T(128)} %param.19) | copy-start | bytes 1540
where the time goes:
time: 110 us; the launch traced here: 109 us
  local copies, waits for them, and re-layouts  53.6 us (49%)
  blocking collectives  24 us (22%)
  matrix products  15 us (14%)
  waiting for transfers between devices  7.1 us (6%)
  starting transfers between devices  6.36 us (6%)
  other arithmetic  3.04 us (3%)
    convert_element_type x4, local copies, waits for them, and re-layouts, one_block(): outer.astype(jnp.bfloat16).reshape(n_rows * sub, n_seq * chans * chans)  25.8 us
    another operation x4, local copies, waits for them, and re-layouts  24 us
    all_gather x1, blocking collectives, per_device(): piece = lax.all_gather(right_use, 'res', axis=0, tiled=True)  13.8 us
    dot_general x4, matrix products, one_block(): jnp.einsum('gsic,jgse->ijgce', left_four, block, preferred_element_type=j...  12.9 us
    all_to_all x1, waiting for transfers between devices, per_device(): lax.all_to_all(alignment_states.reshape(aligned_rows_each_shard, position...  7.1 us
    all_to_all x1, starting transfers between devices, per_device(): lax.all_to_all(alignment_states.reshape(aligned_rows_each_shard, position...  6.36 us
    all_gather x1, blocking collectives, per_device(): rows_all = lax.all_gather(left_use, 'col', axis=1, tiled=True)  4.57 us
    all_to_all x1, blocking collectives, per_device(): lax.all_to_all(left_loc, 'seq', split_axis=1, concat_axis=0, tiled=True)  3.75 us
  transfers between devices with their start and end apart: 1, of which 1 were waited for; matrix products, arithmetic and copies ran while one was open for 2% of the time, Pallas kernels for 0%

commit v1 on v0

--- a/solution.py
+++ b/solution.py
@@ -37,14 +37,19 @@
     seq_loc = aligned_rows_each_shard * position_number
     w_both = jnp.concatenate([first_factor_coeffs, second_factor_coeffs], axis=1)
     bias_both = jnp.concatenate([first_factor_offset, second_factor_offset])
-    raw = lax.all_to_all(
+    lift_things_now = lambda in_array, a_name, dim_no, ndim_at: jnp.concatenate(
+        lax.all_to_all(
+            jnp.stack(jnp.split(in_array, lax.axis_size(a_name), axis=dim_no), 0), a_name, 0, 0
+        ),
+        axis=ndim_at,
+    )
+    raw = lift_things_now(
         alignment_states.reshape(
             aligned_rows_each_shard, position_number, positions_each_shard * hidden_dimension
         ),
-        "res",
-        split_axis=1,
-        concat_axis=0,
-        tiled=True,
+        a_name="res",
+        dim_no=1,
+        ndim_at=0,
     )
     both = project_both(
         raw.reshape(seq_loc * positions_each_shard, hidden_dimension),

time: 110 us -> 111 us (level)
  no operation moved by 1% of the time
where the time goes in v1:
time: 111 us; the launch traced here: 110 us
  local copies, waits for them, and re-layouts  53.6 us (48%)
  blocking collectives  24 us (22%)
  matrix products  15 us (14%)
  waiting for transfers between devices  7.1 us (6%)
  starting transfers between devices  6.36 us (6%)
  other arithmetic  3.74 us (3%)
    convert_element_type x4, local copies, waits for them, and re-layouts, one_block(): outer.astype(jnp.bfloat16).reshape(n_rows * sub, n_seq * chans * chans)  25.8 us
    another operation x4, local copies, waits for them, and re-layouts  24 us
    all_gather x1, blocking collectives, per_device(): piece = lax.all_gather(right_use, 'res', axis=0, tiled=True)  13.8 us
    dot_general x4, matrix products, one_block(): jnp.einsum('gsic,jgse->ijgce', left_four, block, preferred_element_type=j...  12.9 us
    all_to_all x1, waiting for transfers between devices, per_device(): lax.all_to_all(jnp.stack(jnp.split(in_array, lax.axis_size(a_name), axis=...  7.1 us
    all_to_all x1, starting transfers between devices, per_device(): lax.all_to_all(jnp.stack(jnp.split(in_array, lax.axis_size(a_name), axis=...  6.36 us
    all_gather x1, blocking collectives, per_device(): rows_all = lax.all_gather(left_use, 'col', axis=1, tiled=True)  4.57 us
    all_to_all x1, blocking collectives, per_device(): lax.all_to_all(left_loc, 'seq', split_axis=1, concat_axis=0, tiled=True)  3.75 us
  transfers between devices with their start and end apart: 1, of which 1 were waited for; matrix products, arithmetic and copies ran while one was open for 2% of the time, Pallas kernels for 0%

profile of v1, /device:TPU:0, one launch (start us, length us, event | category | flops | bytes accessed | tf_op | source)
XLA Modules:
  0.0 110.1 jit_solution(8696647036796812555)
XLA Ops:
  0.0 1.2 %reshape.54 = bf16[8,4,4096]{2,1,0:T(4,128)(2,1)S(1)} reshape(bf16[8,64,256]{2,1,0:T(8,128)(2,1)} %param.11) | data formatting | bytes 524288 | tf_op jit(solution)/shard_map/reshape | solution.py:47
  1.2 0.5 fusion.13
  2.1 0.7 pad_maximum_fusion.1
  2.8 6.4 %all-to-all-start = ((bf16[4,8,1,4096]{3,1,2,0:T(8,128)(2,1)}), bf16[4,8,1,4096]{3,1,2,0:T(8,128)(2,1)S(1)}, u32[]{:S(2)}, u32[]{:S(2)}) async-start(bf16[4,8,1,4096]{3,1,2,0:T(8,128)(2,1)} %pad_maximum_fusion.1), calls=%async_computation | async-start | bytes 524288 | tf_op jit(solution)/shard_map/all_to_all | solution.py:41
  9.2 0.7 pad_maximum_fusion.2
  9.9 1.1 pad_maximum_fusion
  11.0 7.1 %all-to-all-done = bf16[4,8,1,4096]{3,1,2,0:T(8,128)(2,1)S(1)} async-done(((bf16[4,8,1,4096]{3,1,2,0:T(8,128)(2,1)}), bf16[4,8,1,4096]{3,1,2,0:T(8,128)(2,1)S(1)}, u32[]{:S(2)}, u32[]{:S(2)}) %all-to-all-start) | async-done | bytes 262176 | tf_op jit(solution)/shard_map/all_to_all | solution.py:41
  18.3 0.2 multiply_reduce_fusion
  18.6 0.3 fusion.4
  19.4 3.7 %all_to_all.24 = bf16[32,2,256]{2,0,1:T(8,128)(2,1)S(1)} all-to-all(bf16[32,2,256]{2,0,1:T(8,128)(2,1)S(1)} %copy.56), channel_id=1, replica_groups=mesh['groups'=2,'res'=4,'col'=2,'seq'=2] {'seq'}, dimensions={1} | all-to-all | bytes 65536 | tf_op jit(solution)/shard_map/all_to_all | solution.py:65
  23.1 4.6 %all_gather.11 = bf16[64,512]{1,0:T(8,128)(2,1)S(1)} all-gather(bf16[64,256]{1,0:T(8,128)(2,1)S(1)} %bitcast.58), channel_id=1, replica_groups=mesh['groups'=2,'res'=4,'col'=2,'seq'=2] {'col'}, dimensions={1}, use_global_device_ids=true | all-gather | bytes 98304 | tf_op jit(solution)/shard_map/all_gather | solution.py:67
  28.2 1.9 %all_gather.9 = bf16[16,2048]{1,0:T(8,128)(2,1)S(1)} all-gather(bf16[16,1024]{1,0:T(8,128)(2,1)S(1)} %reshape.56), channel_id=1, replica_groups=mesh['groups'=2,'res'=4,'col'=2,'seq'=2] {'seq'}, dimensions={1}, use_global_device_ids=true | all-gather | bytes 98304 | tf_op jit(solution)/shard_map/all_gather | solution.py:66
  30.0 13.8 %all_gather.10 = bf16[64,2048]{1,0:T(8,128)(2,1)S(1)} all-gather(bf16[16,2048]{1,0:T(8,128)(2,1)S(1)} %all_gather.9), channel_id=1, replica_groups=mesh['groups'=2,'res'=4,'col'=2,'seq'=2] {'res'}, dimensions={0}, use_global_device_ids=true | all-gather | bytes 327680 | tf_op jit(solution)/shard_map/all_gather | solution.py:83
  43.8 65.4 %while.10 = (s32[]{:T(128)}, f32[4,16,16,128]{3,2,1,0:T(8,128)S(1)}, bf16[4,16,2048]{2,1,0:T(8,128)(2,1)S(1)}, bf16[2,32,16,32]{3,1,2,0:T(8,128)(2,1)S(1)}, bf16[2048,128]{1,0:T(8,128)(2,1)S(1)}, /*index=5*/s32[]{:T(128)}) while((s32[]{:T(128)}, f32[4,16,16,128]{3,2,1,0:T(8,128)S(1)}, bf16[4,16,2048]{2,1,0:T(8,128)(2,1)S(1)}, ...), condition=%wide.region_3.4_spmd, body=%wide.region_2.3_spmd.sunk | while | flops 168296448 | bytes 7340109 | solution.py:90
  43.8 0.2 reshape.65
  44.0 3.2 %convert_bitcast_fusion.2 = bf16[16,16,2,32,32]{3,4,0,1,2:T(8,128)(2,1)} fusion(bf16[2,32,16,32]{3,1,2,0:T(8,128)(2,1)S(1)} %get-tuple-element.129, bf16[16,2,32,32]{3,2,1,0:T(8,128)(2,1)S(1)} %reshape.65), kind=kOutput, calls=%fused_computation.clone.1 | convolution fusion | flops 34078720 | bytes 1179648 | tf_op jit(solution)/shard_map/while/body/eval_jaxpr/gsic,jgse->ijgce/dot_general | solution.py:78
  47.3 6.5 %copy.76 = bf16[16,16,2,32,32]{4,3,2,1,0:T(8,128)(2,1)} copy(bf16[16,16,2,32,32]{3,4,0,1,2:T(8,128)(2,1)} %convert_bitcast_fusion.2) | data formatting | bytes 2097152 | tf_op jit(solution)/shard_map/while/body/eval_jaxpr/convert_element_type | solution.py:79
  53.7 6.0 %reshape.66 = bf16[16,16,2048]{2,1,0:T(8,128)(2,1)S(1)} reshape(bf16[16,16,2,32,32]{4,3,2,1,0:T(8,128)(2,1)} %copy.76) | data formatting | bytes 2097152 | tf_op jit(solution)/shard_map/reshape.21
  59.7 0.4 fusion.28
  60.4 3.2 %convert_bitcast_fusion.2 = bf16[16,16,2,32,32]{3,4,0,1,2:T(8,128)(2,1)} fusion(bf16[2,32,16,32]{3,1,2,0:T(8,128)(2,1)S(1)} %get-tuple-element.129, bf16[16,2,32,32]{3,2,1,0:T(8,128)(2,1)S(1)} %reshape.65), kind=kOutput, calls=%fused_computation.clone.1 | convolution fusion | flops 34078720 | bytes 1179648 | tf_op jit(solution)/shard_map/while/body/eval_jaxpr/gsic,jgse->ijgce/dot_general | solution.py:78
  63.6 6.5 %copy.76 = bf16[16,16,2,32,32]{4,3,2,1,0:T(8,128)(2,1)} copy(bf16[16,16,2,32,32]{3,4,0,1,2:T(8,128)(2,1)} %convert_bitcast_fusion.2) | data formatting | bytes 2097152 | tf_op jit(solution)/shard_map/while/body/eval_jaxpr/convert_element_type | solution.py:79
  70.1 6.0 %reshape.66 = bf16[16,16,2048]{2,1,0:T(8,128)(2,1)S(1)} reshape(bf16[16,16,2,32,32]{4,3,2,1,0:T(8,128)(2,1)} %copy.76) | data formatting | bytes 2097152 | tf_op jit(solution)/shard_map/reshape.21
  76.1 0.4 fusion.28
  76.7 3.2 %convert_bitcast_fusion.2 = bf16[16,16,2,32,32]{3,4,0,1,2:T(8,128)(2,1)} fusion(bf16[2,32,16,32]{3,1,2,0:T(8,128)(2,1)S(1)} %get-tuple-element.129, bf16[16,2,32,32]{3,2,1,0:T(8,128)(2,1)S(1)} %reshape.65), kind=kOutput, calls=%fused_computation.clone.1 | convolution fusion | flops 34078720 | bytes 1179648 | tf_op jit(solution)/shard_map/while/body/eval_jaxpr/gsic,jgse->ijgce/dot_general | solution.py:78
  80.0 6.5 %copy.76 = bf16[16,16,2,32,32]{4,3,2,1,0:T(8,128)(2,1)} copy(bf16[16,16,2,32,32]{3,4,0,1,2:T(8,128)(2,1)} %convert_bitcast_fusion.2) | data formatting | bytes 2097152 | tf_op jit(solution)/shard_map/while/body/eval_jaxpr/convert_element_type | solution.py:79
  86.4 6.0 %reshape.66 = bf16[16,16,2048]{2,1,0:T(8,128)(2,1)S(1)} reshape(bf16[16,16,2,32,32]{4,3,2,1,0:T(8,128)(2,1)} %copy.76) | data formatting | bytes 2097152 | tf_op jit(solution)/shard_map/reshape.21
  92.4 0.4 fusion.28
  93.1 3.2 %convert_bitcast_fusion.2 = bf16[16,16,2,32,32]{3,4,0,1,2:T(8,128)(2,1)} fusion(bf16[2,32,16,32]{3,1,2,0:T(8,128)(2,1)S(1)} %get-tuple-element.129, bf16[16,2,32,32]{3,2,1,0:T(8,128)(2,1)S(1)} %reshape.65), kind=kOutput, calls=%fused_computation.clone.1 | convolution fusion | flops 34078720 | bytes 1179648 | tf_op jit(solution)/shard_map/while/body/eval_jaxpr/gsic,jgse->ijgce/dot_general | solution.py:78
  96.3 6.5 %copy.76 = bf16[16,16,2,32,32]{4,3,2,1,0:T(8,128)(2,1)} copy(bf16[16,16,2,32,32]{3,4,0,1,2:T(8,128)(2,1)} %convert_bitcast_fusion.2) | data formatting | bytes 2097152 | tf_op jit(solution)/shard_map/while/body/eval_jaxpr/convert_element_type | solution.py:79
  102.7 6.0 %reshape.66 = bf16[16,16,2048]{2,1,0:T(8,128)(2,1)S(1)} reshape(bf16[16,16,2,32,32]{4,3,2,1,0:T(8,128)(2,1)} %copy.76) | data formatting | bytes 2097152 | tf_op jit(solution)/shard_map/reshape.21
  108.8 0.4 fusion.28
  109.3 0.8 add_convert_fusion
  (34 shorter events, 2.1 us)
Async XLA Ops:
  0.0 18.6 %copy-start.4 = (f32[256]{0:T(256)S(1)}, f32[256]{0:T(256)}, u32[]{:S(2)}) copy-start(f32[256]{0:T(256)} %param.12) | copy-start | bytes 3076
  0.0 18.6 %copy-start.3 = (f32[256]{0:T(256)S(1)}, f32[256]{0:T(256)}, u32[]{:S(2)}) copy-start(f32[256]{0:T(256)} %param.13) | copy-start | bytes 3076
  0.0 18.6 %copy-start.2 = (bf16[256,32]{0,1:T(8,128)(2,1)S(1)}, bf16[256,32]{0,1:T(8,128)(2,1)}, u32[]{:S(2)}) copy-start(bf16[256,32]{0,1:T(8,128)(2,1)} %param.14) | copy-start | bytes 49156
  0.0 18.6 %copy-start.1 = (bf16[256,32]{0,1:T(8,128)(2,1)S(1)}, bf16[256,32]{0,1:T(8,128)(2,1)}, u32[]{:S(2)}) copy-start(bf16[256,32]{0,1:T(8,128)(2,1)} %param.16) | copy-start | bytes 49156
  2.8 15.3 %all-to-all-start = ((bf16[4,8,1,4096]{3,1,2,0:T(8,128)(2,1)}), bf16[4,8,1,4096]{3,1,2,0:T(8,128)(2,1)S(1)}, u32[]{:S(2)}, u32[]{:S(2)}) async-start(bf16[4,8,1,4096]{3,1,2,0:T(8,128)(2,1)} %pad_maximum_fusion.1), calls=%async_computation | async-start | bytes 524288 | tf_op jit(solution)/shard_map/all_to_all | solution.py:41
  43.8 65.5 %copy-start = (f32[128]{0:T(128)S(1)}, f32[128]{0:T(128)}, u32[]{:S(2)}) copy-start(f32[128]{0:T(128)} %param.19) | copy-start | bytes 1540
